TPU v7x, 512 devices: a whole 4x8x8 slice. The times are simulated.
512 devices in a mesh: wide: 64 (over z, y_hi, core), narrow: 8 (over x, y_lo).
Axes of the slice: x: 4, y: 8 (y_hi: 4, y_lo: 2; y = y_hi * 2 + y_lo), z: 8, core: 2. Of those that a mesh axis runs over, the one named last changes fastest.
Arguments:
- positions: float32 [3, 131072], P(None, ('wide', 'narrow')), may hold values from 0 to 1
- volumes: float32 [131072], P(('wide', 'narrow')), may hold values from 0.5 to 2
- phase_field: float32 [131072], P(('wide', 'narrow')), may hold values from -1 to 1.4
- stencil_weights: float32 [64, 131072], P(None, ('wide', 'narrow')), may hold values from 0.005 to 0.05
- stencil_slots: int32 [64, 131072], P(None, ('wide', 'narrow')), may hold values from 0 to 767, as said below
- send_lists: int32 [2, 131072], P(None, ('wide', 'narrow')), may hold values from 0 to 255, as said below
Outputs:
- phase_next: float32 [131072], P(('wide', 'narrow'))
- potential_next: float32 [131072], P(('wide', 'narrow'))
Inputs may be any that keep to these rules, and one draw needn't show every extreme that they name: `stencil_slots`: entry k of point i names a neighbour in ext of i's block: values below 256 are rows of the same block other than i; 256 + s is slot s of the list that the block one lower along wide (cyclically) sends up, 512 + s slot s of the list that the block one higher sends down; s is always below that list's count c, and every slot below c is named by some point of the receiving block. `send_lists`: each block's list in each row has a count c of 1 to 256: its first c slots hold distinct rows of 0 to 255 and the rest hold 0; in each row some block's list is full.
All inputs are finite; a program needn't handle non-finite values.
Results may differ from a plain program's by a relative error of at most 0.00002.
Values sent between devices are 32-bit elements; how exact they have to be, the bound alone decides.
A program may use at most 64 MiB of HBM per device.

v0:
```python
import jax
import jax.numpy as jnp
from jax import lax
from jax.sharding import PartitionSpec as P

kernel_strength = 0.1
gradient_energy = 0.5
time_step = 0.2


def padded(cells, sides, width):
    for axis, dim in sides:
        count = lax.axis_size(axis)
        head = lax.slice_in_dim(cells, 0, width, axis=dim)
        tail = lax.slice_in_dim(cells, cells.shape[dim] - width, cells.shape[dim], axis=dim)
        cells = jnp.concatenate(
            [
                lax.ppermute(tail, axis, [(i, (i + 1) % count) for i in range(count)]),
                cells,
                lax.ppermute(head, axis, [((i + 1) % count, i) for i in range(count)]),
            ],
            axis=dim,
        )
    return cells


def add_sources(totals, targets, sources, vols, values, kernel_decay):
    count_src = values.shape[0]
    block_len = 512

    def add_block(turn, partial_sums):
        offset = turn * block_len
        src_block = lax.dynamic_slice_in_dim(sources, offset, block_len, 1)
        vol_block = lax.dynamic_slice_in_dim(vols, offset, block_len, 0)
        val_block = lax.dynamic_slice_in_dim(values, offset, block_len, 0)
        distance = (targets[0][:, None] - src_block[0][None, :]) ** 2
        distance = distance + (targets[1][:, None] - src_block[1][None, :]) ** 2
        distance = distance + (targets[2][:, None] - src_block[2][None, :]) ** 2
        gauss_vol = jnp.exp(-kernel_decay * distance) * vol_block[None, :]
        return (
            partial_sums[0] + jnp.sum(gauss_vol, axis=1),
            partial_sums[1] + jnp.sum(gauss_vol * val_block[None, :], axis=1),
        )

    return lax.fori_loop(0, count_src // block_len, add_block, totals)


def shards(positions, volumes, phase_field, stencil_weights, stencil_slots, send_lists):
    own_rows = phase_field.shape[0]
    send_len = send_lists.shape[1]
    patch_len = own_rows * lax.axis_size("narrow")
    kernel_decay = 0.5 * float(patch_len) ** (2.0 / 3.0)
    packet_rows = jnp.concatenate([send_lists[1], send_lists[0]])

    def extend(field_now):
        rim_values = padded(field_now[packet_rows], (("wide", 0),), send_len)
        return jnp.concatenate([field_now, rim_values[:send_len], rim_values[-send_len:]])

    zero_sums = (jnp.zeros((own_rows,), jnp.float32), jnp.zeros((own_rows,), jnp.float32))

    def kernel_totals(field_now):
        stacked = jnp.concatenate([positions, volumes[None, :], field_now[None, :]], axis=0)
        part_rows = lax.all_gather(stacked, "narrow", axis=1, tiled=True)
        return add_sources(
            zero_sums, positions, part_rows[:3], part_rows[3], part_rows[4], kernel_decay
        )

    def laplace(field_now):
        extended = extend(field_now)
        neighbour_vals = extended[stencil_slots]
        return jnp.sum(stencil_weights * (neighbour_vals - field_now[None, :]), axis=0)

    def potential(field_now):
        sum_mass, sum_field = kernel_totals(field_now)
        kernel_term = kernel_strength * sum_mass * field_now - kernel_strength * sum_field
        return field_now**3 - field_now + kernel_term - gradient_energy * laplace(field_now)

    potential_now = potential(phase_field)
    phase_next = phase_field + time_step * laplace(potential_now)
    return (phase_next, potential(phase_next))


def solution(mesh):
    placed = (
        P(None, ("wide", "narrow")),
        P(("wide", "narrow")),
        P(("wide", "narrow")),
        P(None, ("wide", "narrow")),
        P(None, ("wide", "narrow")),
        P(None, ("wide", "narrow")),
    )
    return jax.shard_map(
        shards,
        mesh=mesh,
        in_specs=placed,
        out_specs=(P(("wide", "narrow")), P(("wide", "narrow"))),
        check_vma=False,
    )
```

profile of v0, /device:TPU:8, one launch (start us, length us, event | category | flops | bytes accessed | tf_op | source)
XLA Modules:
  0.0 310.8 jit_solution(3009720424811803415)
XLA Ops:
  0.6 0.8 slice_bitcast_fusion.1
  1.4 0.7 copy-done
  2.1 3.5 %gather_fusion = f32[512]{0:T(512)S(1)} fusion(f32[256]{0:T(256)S(1)} %copy-done, s32[1024]{0:T(1024)S(1)} %pad_clamp_fusion), kind=kCustom, calls=%fused_computation | custom fusion | bytes 6144 | tf_op jit(solution)/shard_map/gather | solution.py:56
  5.6 1.9 collective-permute-start
  7.5 13.2 %collective-permute-start.1 = (f32[256]{0:T(256)S(1)}, f32[256]{0:T(256)S(1)}, u32[]{:S(2)}, u32[]{:S(2)}) collective-permute-start(f32[256]{0:T(256)S(1)} %get-tuple-element.361), channel_id=1, source_target_pairs={{8,0},{16,8},{24,16},{32,24},{40,32},{48,40},{56,48},{64,56},{72,6... | collective-permute-start | bytes 3080 | tf_op jit(solution)/shard_map/ppermute | solution.py:20
  20.7 0.7 copy-done.6
  21.4 28.3 %all_gather.6 = f32[5,2048]{1,0:T(8,128)S(1)} all-gather(f32[5,256]{1,0:T(8,128)S(1)} %pad_maximum_fusion), channel_id=1, replica_groups=mesh['wide'=64,'narrow'=8] {'narrow'}, dimensions={1}, use_global_device_ids=true | all-gather | bytes 46080 | tf_op jit(solution)/shard_map/all_gather | solution.py:63
  49.8 0.6 copy-done.4
  50.7 0.7 slice-done
  51.4 2.8 while.32
  54.2 65.3 %gather_fusion.1 = f32[16384]{0:T(1024)S(1)} fusion(f32[768]{0:T(1024)S(1)} %pad_maximum_fusion.2, s32[16384]{0:T(1024)S(1)} %broadcast_clamp_fusion), kind=kCustom, calls=%fused_computation.1 | custom fusion | bytes 196608 | tf_op jit(solution)/shard_map/gather | solution.py:70
  119.6 0.8 copy-done.2
  120.4 3.5 %gather_fusion.2 = f32[512]{0:T(512)S(1)} fusion(f32[256]{0:T(256)S(1)} %fusion.5, s32[1024]{0:T(1024)S(1)} %pad_clamp_fusion), kind=kCustom, calls=%fused_computation.2 | custom fusion | bytes 6144 | tf_op jit(solution)/shard_map/gather | solution.py:56
  123.9 1.9 collective-permute-start.2
  125.9 7.9 %collective-permute-start.3 = (f32[256]{0:T(256)S(1)}, f32[256]{0:T(256)S(1)}, u32[]{:S(2)}, u32[]{:S(2)}) collective-permute-start(f32[256]{0:T(256)S(1)} %get-tuple-element.359), channel_id=1, source_target_pairs={{8,0},{16,8},{24,16},{32,24},{40,32},{48,40},{56,48},{64,56},{72,6... | collective-permute-start | bytes 3080 | tf_op jit(solution)/shard_map/ppermute | solution.py:20
  133.8 1.2 collective-permute-done.3
  135.0 65.3 %gather_fusion.3 = f32[16384]{0:T(1024)S(1)} fusion(f32[768]{0:T(1024)S(1)} %pad_maximum_fusion.3, s32[16384]{0:T(1024)S(1)} %broadcast_clamp_fusion), kind=kCustom, calls=%fused_computation.3 | custom fusion | bytes 196608 | tf_op jit(solution)/shard_map/gather | solution.py:70
  200.4 28.3 %all_gather.7 = f32[5,2048]{1,0:T(8,128)S(1)} all-gather(f32[5,256]{1,0:T(8,128)S(1)} %fusion.3), channel_id=1, replica_groups=mesh['wide'=64,'narrow'=8] {'narrow'}, dimensions={1}, use_global_device_ids=true | all-gather | bytes 46080 | tf_op jit(solution)/shard_map/all_gather | solution.py:63
  228.7 3.5 %gather_fusion.4 = f32[512]{0:T(512)S(1)} fusion(f32[256]{0:T(256)S(1)} %multiply_add_fusion, s32[1024]{0:T(1024)S(1)} %pad_clamp_fusion), kind=kCustom, calls=%fused_computation.4 | custom fusion | bytes 6144 | tf_op jit(solution)/shard_map/gather | solution.py:56
  232.2 1.9 collective-permute-start.4
  234.1 7.9 %collective-permute-start.5 = (f32[256]{0:T(256)S(1)}, f32[256]{0:T(256)S(1)}, u32[]{:S(2)}, u32[]{:S(2)}) collective-permute-start(f32[256]{0:T(256)S(1)} %get-tuple-element.357), channel_id=1, source_target_pairs={{8,0},{16,8},{24,16},{32,24},{40,32},{48,40},{56,48},{64,56},{72,6... | collective-permute-start | bytes 3080 | tf_op jit(solution)/shard_map/ppermute | solution.py:20
  242.0 2.8 while.33
  244.9 65.3 %gather_fusion.5 = f32[16384]{0:T(1024)S(1)} fusion(f32[768]{0:T(1024)S(1)} %pad_maximum_fusion.4, s32[16384]{0:T(1024)S(1)} %broadcast_clamp_fusion), kind=kCustom, calls=%fused_computation.5 | custom fusion | bytes 196608 | tf_op jit(solution)/shard_map/gather | solution.py:70
  310.2 0.6 fusion.7
  (92 shorter events, 6.1 us)
Async XLA Ops:
  1.4 0.7 copy-start
  5.6 15.1 %copy-start.3 = (f32[3,256]{1,0:T(4,128)S(1)}, f32[3,256]{1,0:T(4,128)}, u32[]{:S(2)}) copy-start(f32[3,256]{1,0:T(4,128)} %param.10) | copy-start | bytes 9220
  5.6 48.6 %collective-permute-start = (f32[256]{0:T(256)S(1)}, f32[256]{0:T(256)S(1)}, u32[]{:S(2)}, u32[]{:S(2)}) collective-permute-start(f32[256]{0:T(256)S(1)} %get-tuple-element.360), channel_id=1, source_target_pairs={{0,8},{8,16},{16,24},{24,32},{32,40},{40,48},{48,56},{56,64},{64,7... | collective-permute-start | bytes 3080 | tf_op jit(solution)/shard_map/ppermute | solution.py:18
  7.5 46.7 %collective-permute-start.1 = (f32[256]{0:T(256)S(1)}, f32[256]{0:T(256)S(1)}, u32[]{:S(2)}, u32[]{:S(2)}) collective-permute-start(f32[256]{0:T(256)S(1)} %get-tuple-element.361), channel_id=1, source_target_pairs={{8,0},{16,8},{24,16},{32,24},{40,32},{48,40},{56,48},{64,56},{72,6... | collective-permute-start | bytes 3080 | tf_op jit(solution)/shard_map/ppermute | solution.py:20
  20.7 0.7 copy-start.6
  49.7 0.6 copy-start.4
  49.7 0.9 copy-start.5
  50.6 0.7 slice-start
  119.5 0.8 copy-start.2
  123.9 9.8 %collective-permute-start.2 = (f32[256]{0:T(256)S(1)}, f32[256]{0:T(256)S(1)}, u32[]{:S(2)}, u32[]{:S(2)}) collective-permute-start(f32[256]{0:T(256)S(1)} %get-tuple-element.358), channel_id=1, source_target_pairs={{0,8},{8,16},{16,24},{24,32},{32,40},{40,48},{48,56},{56,64},{64,7... | collective-permute-start | bytes 3080 | tf_op jit(solution)/shard_map/ppermute | solution.py:18
  125.9 9.1 %collective-permute-start.3 = (f32[256]{0:T(256)S(1)}, f32[256]{0:T(256)S(1)}, u32[]{:S(2)}, u32[]{:S(2)}) collective-permute-start(f32[256]{0:T(256)S(1)} %get-tuple-element.359), channel_id=1, source_target_pairs={{8,0},{16,8},{24,16},{32,24},{40,32},{48,40},{56,48},{64,56},{72,6... | collective-permute-start | bytes 3080 | tf_op jit(solution)/shard_map/ppermute | solution.py:20
  200.3 109.9 %copy-start.1 = (f32[256]{0:T(256)}, f32[256]{0:T(256)S(1)}, u32[]{:S(2)}) copy-start(f32[256]{0:T(256)S(1)} %multiply_add_fusion) | copy-start | bytes 3076
  232.2 12.7 %collective-permute-start.4 = (f32[256]{0:T(256)S(1)}, f32[256]{0:T(256)S(1)}, u32[]{:S(2)}, u32[]{:S(2)}) collective-permute-start(f32[256]{0:T(256)S(1)} %get-tuple-element.356), channel_id=1, source_target_pairs={{0,8},{8,16},{16,24},{24,32},{32,40},{40,48},{48,56},{56,64},{64,7... | collective-permute-start | bytes 3080 | tf_op jit(solution)/shard_map/ppermute | solution.py:18
  234.1 10.7 %collective-permute-start.5 = (f32[256]{0:T(256)S(1)}, f32[256]{0:T(256)S(1)}, u32[]{:S(2)}, u32[]{:S(2)}) collective-permute-start(f32[256]{0:T(256)S(1)} %get-tuple-element.357), channel_id=1, source_target_pairs={{8,0},{16,8},{24,16},{32,24},{40,32},{48,40},{56,48},{64,56},{72,6... | collective-permute-start | bytes 3080 | tf_op jit(solution)/shard_map/ppermute | solution.py:20
where the time goes:
time: 311 us
  local copies, waits for them, and re-layouts  213 us (68%)
  blocking collectives  56.6 us (18%)
  starting transfers between devices  34.7 us (11%)
  other arithmetic  4.31 us (1%)
    gather x6, local copies, waits for them, and re-layouts, laplace(): neighbour_vals = extended[stencil_slots]  196 us
    all_gather x2, blocking collectives, kernel_totals(): part_rows = lax.all_gather(stacked, 'narrow', axis=1, tiled=True)  56.6 us
    ppermute x3, starting transfers between devices, padded(): lax.ppermute(head, axis, [((i + 1) % count, i) for i in range(count)])  28.9 us
    gather x3, local copies, waits for them, and re-layouts, extend(): rim_values = padded(field_now[packet_rows], (('wide', 0),), send_len)  10.5 us
  transfers between devices with their start and end apart: 6, of which 1 were waited for; matrix products, arithmetic and copies ran while one was open for 2% of the time, Pallas kernels for 0%

commit v1 on v0

--- a/solution.py
+++ b/solution.py
@@ -60,7 +60,9 @@
 
     def kernel_totals(field_now):
         stacked = jnp.concatenate([positions, volumes[None, :], field_now[None, :]], axis=0)
-        part_rows = lax.all_gather(stacked, "narrow", axis=1, tiled=True)
+        part_rows = jnp.concatenate(
+            lax.all_to_all(jnp.stack([stacked] * lax.axis_size("narrow")), "narrow", 0, 0), axis=1
+        )
         return add_sources(
             zero_sums, positions, part_rows[:3], part_rows[3], part_rows[4], kernel_decay
         )

time: 311 us -> 266 us (0.86)
  the two profiles are of different devices: /device:TPU:8 before, /device:TPU:2 now
where the time goes in v1:
time: 266 us
  local copies, waits for them, and re-layouts  212 us (80%)
  starting transfers between devices  46.3 us (17%)
  other arithmetic  4.3 us (2%)
    gather x6, local copies, waits for them, and re-layouts, laplace(): neighbour_vals = extended[stencil_slots]  196 us
    ppermute x3, starting transfers between devices, padded(): lax.ppermute(head, axis, [((i + 1) % count, i) for i in range(count)])  29.8 us
    all_to_all x2, starting transfers between devices, kernel_totals(): lax.all_to_all(jnp.stack([stacked] * lax.axis_size('narrow')), 'narrow',...  10.8 us
    gather x3, local copies, waits for them, and re-layouts, extend(): rim_values = padded(field_now[packet_rows], (('wide', 0),), send_len)  10.5 us
    ppermute x3, starting transfers between devices, padded(): lax.ppermute(tail, axis, [(i, (i + 1) % count) for i in range(count)])  5.76 us
  transfers between devices with their start and end apart: 8, of which 1 were waited for; matrix products, arithmetic and copies ran while one was open for 50% of the time, Pallas kernels for 0%

profile of v1, /device:TPU:2, one launch (start us, length us, event | category | flops | bytes accessed | tf_op | source)
XLA Modules:
  0.0 265.6 jit_solution(15991493932549470355)
XLA Ops:
  0.6 0.8 slice_bitcast_fusion.1
  1.4 0.7 copy-done
  2.1 3.5 %gather_fusion = f32[512]{0:T(512)S(1)} fusion(f32[256]{0:T(256)S(1)} %copy-done, s32[1024]{0:T(1024)S(1)} %pad_clamp_fusion), kind=kCustom, calls=%fused_computation | custom fusion | bytes 6144 | tf_op jit(solution)/shard_map/gather | solution.py:56
  5.6 1.9 collective-permute-start
  7.5 14.1 %collective-permute-start.1 = (f32[256]{0:T(256)S(1)}, f32[256]{0:T(256)S(1)}, u32[]{:S(2)}, u32[]{:S(2)}) collective-permute-start(f32[256]{0:T(256)S(1)} %get-tuple-element.361), channel_id=1, source_target_pairs={{8,0},{16,8},{24,16},{32,24},{40,32},{48,40},{56,48},{64,56},{72,6... | collective-permute-start | bytes 3080 | tf_op jit(solution)/shard_map/ppermute | solution.py:20
  21.6 0.7 copy-done.5
  22.3 0.6 stack.4
  22.9 5.1 %all-to-all-start = ((f32[8,5,256]{2,1,0:T(8,128)}), f32[8,5,256]{2,1,0:T(8,128)S(1)}, u32[]{:S(2)}, u32[]{:S(2)}) async-start(f32[8,5,256]{2,1,0:T(8,128)} %stack.4), calls=%async_computation | async-start | bytes 131072 | tf_op jit(solution)/shard_map/all_to_all | solution.py:64
  28.2 65.3 %gather_fusion.1 = f32[16384]{0:T(1024)S(1)} fusion(f32[768]{0:T(1024)S(1)} %pad_maximum_fusion.2, s32[16384]{0:T(1024)S(1)} %broadcast_clamp_fusion), kind=kCustom, calls=%fused_computation.1 | custom fusion | bytes 196608 | tf_op jit(solution)/shard_map/gather | solution.py:72
  93.5 0.8 copy-done.2
  94.3 2.8 %while.32 = (s32[]{:T(128)}, f32[256]{0:T(256)S(1)}, f32[256]{0:T(256)S(1)}, f32[3,256]{1,0:T(4,128)S(1)}, f32[3,2048]{1,0:T(4,128)S(1)}, /*index=5*/f32[2048]{0...) while((s32[]{:T(128)}, f32[256]{0:T(256)S(1)}, ...), condition=%wide.region_3.0_spmd.clone, body=%wide.region_0.0_spmd.clone.sunk | while | flops 1704457 | bytes 48361 | solution.py:45
  97.2 3.5 %gather_fusion.2 = f32[512]{0:T(512)S(1)} fusion(f32[256]{0:T(256)S(1)} %fusion.5, s32[1024]{0:T(1024)S(1)} %pad_clamp_fusion), kind=kCustom, calls=%fused_computation.2 | custom fusion | bytes 6144 | tf_op jit(solution)/shard_map/gather | solution.py:56
  100.7 1.9 collective-permute-start.2
  102.6 7.9 %collective-permute-start.3 = (f32[256]{0:T(256)S(1)}, f32[256]{0:T(256)S(1)}, u32[]{:S(2)}, u32[]{:S(2)}) collective-permute-start(f32[256]{0:T(256)S(1)} %get-tuple-element.359), channel_id=1, source_target_pairs={{8,0},{16,8},{24,16},{32,24},{40,32},{48,40},{56,48},{64,56},{72,6... | collective-permute-start | bytes 3080 | tf_op jit(solution)/shard_map/ppermute | solution.py:20
  110.5 1.2 collective-permute-done.3
  111.8 65.3 %gather_fusion.3 = f32[16384]{0:T(1024)S(1)} fusion(f32[768]{0:T(1024)S(1)} %pad_maximum_fusion.3, s32[16384]{0:T(1024)S(1)} %broadcast_clamp_fusion), kind=kCustom, calls=%fused_computation.3 | custom fusion | bytes 196608 | tf_op jit(solution)/shard_map/gather | solution.py:72
  177.1 3.5 %gather_fusion.4 = f32[512]{0:T(512)S(1)} fusion(f32[256]{0:T(256)S(1)} %multiply_add_fusion, s32[1024]{0:T(1024)S(1)} %pad_clamp_fusion), kind=kCustom, calls=%fused_computation.4 | custom fusion | bytes 6144 | tf_op jit(solution)/shard_map/gather | solution.py:56
  180.7 1.9 collective-permute-start.4
  182.6 7.9 %collective-permute-start.5 = (f32[256]{0:T(256)S(1)}, f32[256]{0:T(256)S(1)}, u32[]{:S(2)}, u32[]{:S(2)}) collective-permute-start(f32[256]{0:T(256)S(1)} %get-tuple-element.357), channel_id=1, source_target_pairs={{8,0},{16,8},{24,16},{32,24},{40,32},{48,40},{56,48},{64,56},{72,6... | collective-permute-start | bytes 3080 | tf_op jit(solution)/shard_map/ppermute | solution.py:20
  190.5 0.6 stack.5
  191.1 5.7 %all-to-all-start.1 = ((f32[8,5,256]{2,1,0:T(8,128)}), f32[8,5,256]{2,1,0:T(8,128)S(1)}, u32[]{:S(2)}, u32[]{:S(2)}) async-start(f32[8,5,256]{2,1,0:T(8,128)} %stack.5), calls=%async_computation.1 | async-start | bytes 131072 | tf_op jit(solution)/shard_map/all_to_all | solution.py:64
  196.8 65.3 %gather_fusion.5 = f32[16384]{0:T(1024)S(1)} fusion(f32[768]{0:T(1024)S(1)} %pad_maximum_fusion.4, s32[16384]{0:T(1024)S(1)} %broadcast_clamp_fusion), kind=kCustom, calls=%fused_computation.5 | custom fusion | bytes 196608 | tf_op jit(solution)/shard_map/gather | solution.py:72
  262.2 2.8 %while.33 = (s32[]{:T(128)}, f32[256]{0:T(256)S(1)}, f32[256]{0:T(256)S(1)}, f32[3,256]{1,0:T(4,128)S(1)}, f32[3,2048]{1,0:T(4,128)S(1)}, /*index=5*/f32[2048]{0...) while((s32[]{:T(128)}, f32[256]{0:T(256)S(1)}, ...), condition=%wide.region_9.0_spmd.clone, body=%wide.region_6.0_spmd.clone.sunk | while | flops 1704457 | bytes 48361 | solution.py:45
  265.0 0.6 fusion.7
  (93 shorter events, 5.8 us)
Async XLA Ops:
  1.4 0.7 copy-start
  5.6 16.0 %copy-start.3 = (f32[3,256]{1,0:T(4,128)S(1)}, f32[3,256]{1,0:T(4,128)}, u32[]{:S(2)}) copy-start(f32[3,256]{1,0:T(4,128)} %param.10) | copy-start | bytes 9220
  5.6 22.5 %collective-permute-start = (f32[256]{0:T(256)S(1)}, f32[256]{0:T(256)S(1)}, u32[]{:S(2)}, u32[]{:S(2)}) collective-permute-start(f32[256]{0:T(256)S(1)} %get-tuple-element.360), channel_id=1, source_target_pairs={{0,8},{8,16},{16,24},{24,32},{32,40},{40,48},{48,56},{56,64},{64,7... | collective-permute-start | bytes 3080 | tf_op jit(solution)/shard_map/ppermute | solution.py:18
  7.5 20.6 %collective-permute-start.1 = (f32[256]{0:T(256)S(1)}, f32[256]{0:T(256)S(1)}, u32[]{:S(2)}, u32[]{:S(2)}) collective-permute-start(f32[256]{0:T(256)S(1)} %get-tuple-element.361), channel_id=1, source_target_pairs={{8,0},{16,8},{24,16},{32,24},{40,32},{48,40},{56,48},{64,56},{72,6... | collective-permute-start | bytes 3080 | tf_op jit(solution)/shard_map/ppermute | solution.py:20
  21.6 0.7 copy-start.5
  22.9 5.1 %copy-start.4 = (s32[64,256]{1,0:T(8,128)S(1)}, s32[64,256]{1,0:T(8,128)}, u32[]{:S(2)}) copy-start(s32[64,256]{1,0:T(8,128)} %param.14) | copy-start | bytes 196612
  22.9 71.4 %all-to-all-start = ((f32[8,5,256]{2,1,0:T(8,128)}), f32[8,5,256]{2,1,0:T(8,128)S(1)}, u32[]{:S(2)}, u32[]{:S(2)}) async-start(f32[8,5,256]{2,1,0:T(8,128)} %stack.4), calls=%async_computation | async-start | bytes 131072 | tf_op jit(solution)/shard_map/all_to_all | solution.py:64
  93.4 0.8 copy-start.2
  100.7 9.8 %collective-permute-start.2 = (f32[256]{0:T(256)S(1)}, f32[256]{0:T(256)S(1)}, u32[]{:S(2)}, u32[]{:S(2)}) collective-permute-start(f32[256]{0:T(256)S(1)} %get-tuple-element.358), channel_id=1, source_target_pairs={{0,8},{8,16},{16,24},{24,32},{32,40},{40,48},{48,56},{56,64},{64,7... | collective-permute-start | bytes 3080 | tf_op jit(solution)/shard_map/ppermute | solution.py:18
  102.6 9.1 %collective-permute-start.3 = (f32[256]{0:T(256)S(1)}, f32[256]{0:T(256)S(1)}, u32[]{:S(2)}, u32[]{:S(2)}) collective-permute-start(f32[256]{0:T(256)S(1)} %get-tuple-element.359), channel_id=1, source_target_pairs={{8,0},{16,8},{24,16},{32,24},{40,32},{48,40},{56,48},{64,56},{72,6... | collective-permute-start | bytes 3080 | tf_op jit(solution)/shard_map/ppermute | solution.py:20
  177.1 87.9 %copy-start.1 = (f32[256]{0:T(256)}, f32[256]{0:T(256)S(1)}, u32[]{:S(2)}) copy-start(f32[256]{0:T(256)S(1)} %multiply_add_fusion) | copy-start | bytes 3076
  180.7 16.1 %collective-permute-start.4 = (f32[256]{0:T(256)S(1)}, f32[256]{0:T(256)S(1)}, u32[]{:S(2)}, u32[]{:S(2)}) collective-permute-start(f32[256]{0:T(256)S(1)} %get-tuple-element.356), channel_id=1, source_target_pairs={{0,8},{8,16},{16,24},{24,32},{32,40},{40,48},{48,56},{56,64},{64,7... | collective-permute-start | bytes 3080 | tf_op jit(solution)/shard_map/ppermute | solution.py:18
  182.6 14.2 %collective-permute-start.5 = (f32[256]{0:T(256)S(1)}, f32[256]{0:T(256)S(1)}, u32[]{:S(2)}, u32[]{:S(2)}) collective-permute-start(f32[256]{0:T(256)S(1)} %get-tuple-element.357), channel_id=1, source_target_pairs={{8,0},{16,8},{24,16},{32,24},{40,32},{48,40},{56,48},{64,56},{72,6... | collective-permute-start | bytes 3080 | tf_op jit(solution)/shard_map/ppermute | solution.py:20
  191.1 71.1 %all-to-all-start.1 = ((f32[8,5,256]{2,1,0:T(8,128)}), f32[8,5,256]{2,1,0:T(8,128)S(1)}, u32[]{:S(2)}, u32[]{:S(2)}) async-start(f32[8,5,256]{2,1,0:T(8,128)} %stack.5), calls=%async_computation.1 | async-start | bytes 131072 | tf_op jit(solution)/shard_map/all_to_all | solution.py:64
